TPU v7x, 256 devices: a whole 4x4x8 slice. The times are simulated.
256 devices in a mesh: param: 64 (over x, z, y_hi), sensor: 4 (over y_lo, core).
Axes of the slice: x: 4, y: 4 (y_hi: 2, y_lo: 2; y = y_hi * 2 + y_lo), z: 8, core: 2. Of those that a mesh axis runs over, the one named last changes fastest.
Arguments:
- readings: bfloat16 [64, 600, 128], P('param', 'sensor'), may hold values from -6 to 6
- spectra: bfloat16 [2, 65, 600, 8192], P(None, None, 'sensor', 'param'), may hold values from -0.0625 to 0.0625
- stiffness: float32 [8192], P('param'), may hold values from 0.04 to 0.24
Outputs:
- hessian_panel: float32 [64, 600, 128], P('param', 'sensor')
All inputs are finite; a program needn't handle non-finite values.
Results may differ from a plain program's by a relative error of at most 0.0025.
Values may be sent and summed in bfloat16 or wider, within the bound.
No kernel may reach another device: no remote copies, remote signals or barrier semaphores. Data moves between devices by JAX's collectives and lax.ppermute only.
A program may use at most 128 MiB of HBM per device.

v0:
```python
import math

import jax
import jax.numpy as jnp
from jax import lax
from jax.sharding import PartitionSpec as P

STEPS = 64
GY = 64
NCOL = 128


def with_halo(block, sides, width):
    for axis, dim in sides:
        count = lax.axis_size(axis)
        forward = [(i, i + 1) for i in range(count - 1)]
        backward = [(target, source) for source, target in forward]
        low = lax.ppermute(
            lax.slice_in_dim(block, block.shape[dim] - width, None, axis=dim), axis, forward
        )
        high = lax.ppermute(lax.slice_in_dim(block, 0, width, axis=dim), axis, backward)
        block = jnp.concatenate([low, block, high], axis=dim)
    return block


def angles(bins, times):
    prod = bins[:, None] * times[None, :] % (2 * STEPS)
    return prod.astype(jnp.float32) * (2.0 * math.pi / (2 * STEPS))


def accumulate(loop_carry, piece):
    count = piece.shape[0]
    bins = jnp.arange(STEPS + 1, dtype=jnp.int32)
    times = jnp.arange(count, dtype=jnp.int32)
    phase_angle = angles(bins, times)
    scale_factor = 1.0 / math.sqrt(STEPS)
    value_entries = piece.astype(jnp.float32)
    hessian_product = lax.Precision.HIGHEST
    real_part = jnp.einsum(
        "uo,ojm->ujm", jnp.cos(phase_angle) * scale_factor, value_entries, precision=hessian_product
    )
    imaginary_part = loop_carry[1] - jnp.einsum(
        "uo,ojm->ujm", jnp.sin(phase_angle) * scale_factor, value_entries, precision=hessian_product
    )
    return (real_part, imaginary_part)


def inverse_rows(real_part, imaginary_part, count):
    bins = jnp.arange(STEPS + 1, dtype=jnp.int32)
    times = jnp.arange(count, dtype=jnp.int32)
    phase_angle = angles(bins, times)
    weight = jnp.where((bins == 0) | (bins == STEPS), 1.0, 2.0).astype(jnp.float32)[:, None]
    scale_factor = 1.0 / math.sqrt(STEPS)
    hessian_product = lax.Precision.HIGHEST
    cosine_inverse = (jnp.cos(phase_angle) * weight * scale_factor).T
    sine_inverse = (jnp.sin(phase_angle) * weight * scale_factor).T
    return jnp.einsum(
        "ni,ilj->nlj", cosine_inverse, real_part, precision=hessian_product
    ) - jnp.einsum("ni,ilj->nlj", sine_inverse, imaginary_part, precision=hessian_product)


def sweep_once(grid, coeff):
    padded = with_halo(grid.astype(jnp.bfloat16), (("param", 1),), 1).astype(grid.dtype)
    sides = jnp.pad(grid, ((0, 0), (0, 0), (1, 1), (0, 0)))
    beside_all = padded[:, :-2] + padded[:, 2:] + sides[:, :, :-2] + sides[:, :, 2:]
    return grid + coeff * (beside_all - 4.0 * grid)


def shards(readings, spectra, stiffness):
    sens_rows = readings.shape[1]
    points = spectra.shape[3]
    rows_here = points // GY
    empty_data = jnp.zeros((STEPS + 1, sens_rows, NCOL), jnp.float32)
    data_re, data_im = accumulate(
        (empty_data, empty_data), lax.all_gather(readings, "param", axis=0, tiled=True)
    )
    data_re = data_re.astype(jnp.bfloat16)
    data_im = data_im.astype(jnp.bfloat16)
    spectrum_real = spectra[0]
    spectrum_imaginary = spectra[1]
    f32 = jnp.float32
    adj_re = jnp.einsum(
        "ksm,ksc->kmc", spectrum_real, data_re, preferred_element_type=f32
    ) + jnp.einsum("ksm,ksc->kmc", spectrum_imaginary, data_im, preferred_element_type=f32)
    adj_im = jnp.einsum(
        "ksm,ksc->kmc", spectrum_real, data_im, preferred_element_type=f32
    ) - jnp.einsum("ksm,ksc->kmc", spectrum_imaginary, data_re, preferred_element_type=f32)
    field = inverse_rows(adj_re, adj_im, STEPS)
    grid = field.reshape(STEPS, rows_here, GY, NCOL)
    coeff = stiffness.reshape(rows_here, GY)[None, :, :, None]
    empty_model = jnp.zeros((STEPS + 1, points, NCOL), jnp.float32)
    grid = lax.psum(grid, "sensor")
    for sweep in range(2):
        grid = sweep_once(grid, coeff)
    model_re, model_im = accumulate((empty_model, empty_model), grid.reshape(STEPS, points, NCOL))
    model_re = model_re.astype(jnp.bfloat16)
    model_im = model_im.astype(jnp.bfloat16)
    out_re = jnp.einsum(
        "ksm,kmc->ksc", spectrum_real, model_re, preferred_element_type=f32
    ) - jnp.einsum("ksm,kmc->ksc", spectrum_imaginary, model_im, preferred_element_type=f32)
    out_im = jnp.einsum(
        "ksm,kmc->ksc", spectrum_real, model_im, preferred_element_type=f32
    ) + jnp.einsum("ksm,kmc->ksc", spectrum_imaginary, model_re, preferred_element_type=f32)
    return lax.psum_scatter(
        inverse_rows(out_re, out_im, readings.shape[0] * lax.axis_size("param")),
        "param",
        scatter_dimension=0,
        tiled=True,
    )


def solution(mesh):
    return jax.shard_map(
        shards,
        mesh=mesh,
        in_specs=(P("param", "sensor", None), P(None, None, "sensor", "param"), P("param")),
        out_specs=P("param", "sensor", None),
        check_vma=False,
    )
```

profile of v0, /device:TPU:8, one launch (start us, length us, event | category | flops | bytes accessed | tf_op | source)
XLA Modules:
  0.0 806.9 jit_solution(7636657847180767540)
XLA Ops:
  6.5 0.7 all-gather.2.cloned.1.call-update
  7.3 0.0 all-reduce.5.cloned.1.call-start
  7.3 10.1 %fusion.120 = (bf16[1,65,150,128]{3,0,2,1:T(2,128)(2,1)S(1)}, bf16[1,65,150,128]{3,0,2,1:T(2,128)(2,1)S(1)}) fusion(bf16[2,65,150,128]{3,0,2,1:T(2,128)(2,1)} %param.4), kind=kLoop, calls=%fused_computation.126 | loop fusion | bytes 9984000 | tf_op jit(solution)/shard_map/slice | solution.py:80
  17.5 2.7 copy_bitcast_fusion
  20.2 112.0 %all-gather.2.cloned.1.call-done = bf16[64,150,128]{2,1,0:T(8,128)(2,1)} async-done(((bf16[1,150,128]{2,1,0:T(8,128)(2,1)}), bf16[64,150,128]{2,1,0:T(8,128)(2,1)}) %all-gather.2.cloned.1.call-update) | async-done | bytes 2457616 | tf_op jit(solution)/shard_map/all_gather | solution.py:75
  132.2 4.4 fusion.19
  136.7 1.5 fusion.25
  138.1 1.3 copy-done.2
  139.4 0.8 copy-done.6
  140.2 2.5 fusion.21
  142.8 3.4 fusion.23
  146.2 3.4 subtract_bitcast_fusion.1
  149.6 5.7 copy.33
  155.4 7.6 add_bitcast_fusion.1
  162.9 5.6 copy.32
  168.6 6.0 fusion.43
  174.5 5.6 convolution_subtract_fusion
  180.2 0.0 all-reduce.5.cloned.1.call-update
  180.2 0.0 copy-start.7
  180.2 0.0 reduce-scatter.5.cloned.1.call-start
  180.2 92.4 %all-reduce.5.cloned.1.call-done = f32[64,2,64,128]{3,0,2,1:T(8,128)} async-done(((f32[64,2,64,128]{3,0,2,1:T(8,128)}), f32[64,2,64,128]{3,0,2,1:T(8,128)}) %all-reduce.5.cloned.1.call-update) | async-done | bytes 4194320 | tf_op jit(solution)/shard_map/psum | solution.py:92
  272.6 2.7 convert_element_type.51
  275.3 1.3 copy-done.4
  276.7 1.6 fusion.122
  278.2 6.0 collective-permute-start
  284.2 1.3 collective-permute-start.1
  285.5 0.1 mul.185
  285.6 43.3 %collective-permute-done = bf16[64,1,64,128]{3,0,2,1:T(8,128)(2,1)} collective-permute-done((bf16[64,1,64,128]{3,0,2,1:T(8,128)(2,1)}, bf16[64,1,64,128]{3,0,2,1:T(8,128)(2,1)}, u32[]{:S(2)}, u32[]{:S(2)}) %collective-permute-start) | collective-permute-done | bytes 1048608 | tf_op jit(solution)/shard_map/ppermute | solution.py:18
  328.9 2.5 maximum_convert_fusion
  331.5 1.2 fusion.118
  332.7 0.2 fusion.121
  332.8 6.0 collective-permute-start.2
  338.8 1.3 collective-permute-start.3
  340.1 43.2 %collective-permute-done.2 = bf16[64,1,64,128]{3,0,2,1:T(8,128)(2,1)S(1)} collective-permute-done((bf16[64,1,64,128]{3,0,2,1:T(8,128)(2,1)S(1)}, bf16[64,1,64,128]{3,0,2,1:T(8,128)(2,1)S(1)}, u32[]{:S(2)}, u32[]{:S(2)}) %collective-permute-start.2) | collective-permute-done | bytes 1048608 | tf_op jit(solution)/shard_map/ppermute | solution.py:18
  383.3 0.7 maximum_convert_fusion.1
  384.0 1.1 fusion.10
  385.1 4.7 fusion.39
  389.8 4.4 fusion.36
  394.2 1.5 fusion.28
  395.7 1.5 fusion.24
  397.1 1.5 add_bitcast_fusion
  398.7 5.8 fusion
  404.5 1.6 subtract_bitcast_fusion
  406.1 5.6 fusion.16
  411.7 5.1 copy.38
  416.8 0.0 reduce-scatter.5.cloned.1.call-update
  416.8 381.5 %reduce-scatter.5.cloned.1.call-done = f32[1,150,128]{2,1,0:T(8,128)} async-done(((f32[64,150,128]{2,1,0:T(8,128)}), f32[1,150,128]{2,1,0:T(8,128)}) %reduce-scatter.5.cloned.1.call-update) | async-done | bytes 76816
  798.3 1.6 copy.39
  (16 shorter events, 0.0 us)
Async XLA Ops:
  6.5 125.7 %all-gather.2.cloned.1.call-start = ((), (), s32[]{:S(2)}) async-start(), calls=%async_computation.1 | async-start | bytes 2529280 | tf_op jit(solution)/shard_map/all_gather | solution.py:75
  7.3 265.4 %all-reduce.5.cloned.1.call-start = ((), (), s32[]{:S(2)}) async-start(), calls=%async_computation.2 | async-start | bytes 8388608 | tf_op jit(solution)/shard_map/psum | solution.py:92
  132.2 4.4 copy-start
  136.6 2.8 copy-start.2
  136.7 3.6 copy-start.6
  168.6 6.0 copy-start.3
  180.2 105.3 %copy-start.7 = (f32[128]{0:T(128)S(1)}, f32[128]{0:T(128)}, u32[]{:S(2)}) copy-start(f32[128]{0:T(128)} %param.5) | copy-start | bytes 1540
  180.2 618.1 %reduce-scatter.5.cloned.1.call-start = ((), (), s32[]{:S(2)}) async-start(), calls=%async_computation.3 | async-start | bytes 5058560
  275.3 1.4 copy-start.4
  278.2 50.7 %collective-permute-start = (bf16[64,1,64,128]{3,0,2,1:T(8,128)(2,1)}, bf16[64,1,64,128]{3,0,2,1:T(8,128)(2,1)}, u32[]{:S(2)}, u32[]{:S(2)}) collective-permute-start(bf16[64,1,64,128]{3,0,2,1:T(8,128)(2,1)} %get-tuple-element.11), channel_id=1, source_target_pairs={{0,4},{4,8},{8,12},{12,16},{16,20},{20,24},{24,28},{28,32},{32,36}... | collective-permute-start | bytes 3145736 | tf_op jit(solution)/shard_map/ppermute | solution.py:18
  284.2 44.7 %collective-permute-start.1 = (bf16[64,1,64,128]{3,0,2,1:T(8,128)(2,1)}, bf16[64,1,64,128]{3,0,2,1:T(8,128)(2,1)}, u32[]{:S(2)}, u32[]{:S(2)}) collective-permute-start(bf16[64,1,64,128]{3,0,2,1:T(8,128)(2,1)} %get-tuple-element.12), channel_id=1, source_target_pairs={{4,0},{8,4},{12,8},{16,12},{20,16},{24,20},{28,24},{32,28},{36,32}... | collective-permute-start | bytes 3145736 | tf_op jit(solution)/shard_map/ppermute | solution.py:21
  285.6 45.8 %copy-start.5 = (f32[64,2,64,128]{3,0,2,1:T(8,128)S(1)}, f32[64,2,64,128]{3,0,2,1:T(8,128)}, u32[]{:S(2)}) copy-start(f32[64,2,64,128]{3,0,2,1:T(8,128)} %all-reduce.5.cloned.1.call-done) | copy-start | bytes 12582916
  332.8 50.5 %collective-permute-start.2 = (bf16[64,1,64,128]{3,0,2,1:T(8,128)(2,1)S(1)}, bf16[64,1,64,128]{3,0,2,1:T(8,128)(2,1)S(1)}, u32[]{:S(2)}, u32[]{:S(2)}) collective-permute-start(bf16[64,1,64,128]{3,0,2,1:T(8,128)(2,1)S(1)} %get-tuple-element.9), channel_id=1, source_target_pairs={{0,4},{4,8},{8,12},{12,16},{16,20},{20,24},{24,28},{28,32},{32,36}... | collective-permute-start | bytes 3145736 | tf_op jit(solution)/shard_map/ppermute | solution.py:18
  338.8 44.5 %collective-permute-start.3 = (bf16[64,1,64,128]{3,0,2,1:T(8,128)(2,1)S(1)}, bf16[64,1,64,128]{3,0,2,1:T(8,128)(2,1)S(1)}, u32[]{:S(2)}, u32[]{:S(2)}) collective-permute-start(bf16[64,1,64,128]{3,0,2,1:T(8,128)(2,1)S(1)} %get-tuple-element.10), channel_id=1, source_target_pairs={{4,0},{8,4},{12,8},{16,12},{20,16},{24,20},{28,24},{32,28},{36,32}... | collective-permute-start | bytes 3145736 | tf_op jit(solution)/shard_map/ppermute | solution.py:21
  389.7 4.4 copy-start.1
Sparse Core Ops, SparseCore 0:
  10.8 121.3 all-gather.1
  180.3 92.2 all-reduce.4
  416.9 381.3 reduce-scatter.4
where the time goes:
time: 816 us; the launch traced here: 807 us
  waiting for transfers between devices  673 us (82%)
  matrix products  61 us (7%)
  local copies, waits for them, and re-layouts  36.2 us (4%)
  starting transfers between devices  14.6 us (2%)
  between operations  13.8 us (2%)
    unnamed x4, waiting for transfers between devices  382 us
    all_gather x1, waiting for transfers between devices, shards(): lax.all_gather(readings, 'param', axis=0, tiled=True)  112 us
    psum x1, waiting for transfers between devices, shards(): grid = lax.psum(grid, 'sensor')  92.4 us
    ppermute x2, waiting for transfers between devices, with_halo(): lax.ppermute(lax.slice_in_dim(block, block.shape[dim] - width, None, axis...  86.6 us
  transfers between devices with their start and end apart: 7, of which 5 were waited for; matrix products, arithmetic and copies ran while one was open for 2% of the time, Pallas kernels for 0%

commit v1 on v0

v1 whole, which is shorter than its diff:
```python
import math

import jax
import jax.numpy as jnp
import numpy as np
from jax import lax
from jax.experimental import pallas as pl
from jax.experimental.pallas import tpu as pltpu
from jax.sharding import Mesh, PartitionSpec as P

STEPS = 64
NB = STEPS + 1
GY = 64
NCOL = 128
BF = jnp.bfloat16
F32 = jnp.float32
ROWS = 152
FREQ = 136
PTS = 128


def forward_table(steps):
    bins = np.arange(NB)[:, None]
    angle = 2.0 * math.pi * (bins * np.asarray(steps)[None, :] % (2 * STEPS)) / (2 * STEPS)
    rows = np.concatenate([np.cos(angle), -np.sin(angle)]) / math.sqrt(STEPS)
    return np.pad(rows, ((0, FREQ - 2 * NB), (0, 0))).astype(np.float32)


def inverse_table(steps):
    weight = np.full(NB, 2.0, np.float32)
    weight[[0, STEPS]] = 1.0
    weight = np.pad(np.concatenate([weight, weight]), (0, FREQ - 2 * NB))
    return forward_table(steps).T * weight


def halves(value):
    high = value.astype(BF)
    return high, (value - high.astype(F32)).astype(BF)


def dot(a, b):
    return jnp.dot(a, b, preferred_element_type=F32)


def adjoint_kernel(
    read_ref, fwd_ref, inv_ref, spec_ref, keep_ref, give_ref, time_ref, data_ref, adj_ref, spec, sem
):
    copy = pltpu.make_async_copy(spec_ref, spec, sem)
    copy.start()
    for i in range(STEPS):
        time_ref[pl.ds(i * ROWS, ROWS), :] = read_ref[i].astype(F32)
    high, low = halves(fwd_ref[...])
    fwd = jnp.concatenate([high, low], axis=1)

    def to_bins(i, c):
        s0 = i * 4
        values = [time_ref[pl.ds(s0 + j, STEPS, stride=ROWS), :].astype(BF) for j in range(4)]
        block = jnp.concatenate(values, axis=1)
        result = dot(fwd, jnp.concatenate([block, block], axis=0))
        for j in range(4):
            data_ref[pl.ds(s0 + j, FREQ, stride=ROWS), :] = result[:, j * NCOL : (j + 1) * NCOL]
        return c

    lax.fori_loop(0, ROWS // 4, to_bins, 0)
    copy.wait()
    zero = jnp.zeros((PTS, NCOL), F32)
    for j in range(2 * NB, FREQ):
        adj_ref[pl.ds(j, PTS, stride=FREQ), :] = zero
    sensors = spec.shape[2]

    def one_bin(k):
        real = data_ref[pl.ds(pl.multiple_of(k * ROWS, 8), ROWS), :][:sensors].astype(BF)
        imag = data_ref[pl.ds(pl.multiple_of((k + NB) * ROWS, 8), ROWS), :][:sensors].astype(BF)
        first = jnp.concatenate([real, imag], axis=1)
        second = jnp.concatenate([imag, -real], axis=1)
        dims = (((0,), (0,)), ((), ()))
        result = lax.dot_general(
            spec[0, k], first, dims, preferred_element_type=F32
        ) + lax.dot_general(spec[1, k], second, dims, preferred_element_type=F32)
        adj_ref[pl.ds(k, PTS, stride=FREQ), :] = result[:, :NCOL]
        adj_ref[pl.ds(k + NB, PTS, stride=FREQ), :] = result[:, NCOL:]

    def five_bins(i, c):
        for j in range(5):
            one_bin(i * 5 + j)
        return c

    lax.fori_loop(0, NB // 5, five_bins, 0)
    high, low = halves(inv_ref[...])
    inv = jnp.concatenate([high, high, low], axis=1)

    def to_steps(i, c):
        values = [
            adj_ref[pl.ds(pl.multiple_of((i * 4 + j) * FREQ, 8), FREQ), :] for j in range(4)
        ]
        top, rest = halves(jnp.concatenate(values, axis=1))
        result = dot(inv, jnp.concatenate([top, rest, top], axis=0))
        for j in range(4):
            block = result[:, j * NCOL : (j + 1) * NCOL]
            for p in range(4):
                keep_ref[p, i * 4 + j] = block[8 * p : 8 * p + 8]
                give_ref[p, i * 4 + j] = block[32 + 8 * p : 40 + 8 * p].astype(BF)
        return c

    lax.fori_loop(0, PTS // 4, to_steps, 0)


def adjoint(everything, fwd, inv, spectra):
    vmem = pl.BlockSpec(memory_space=pltpu.VMEM)
    return pl.pallas_call(
        adjoint_kernel,
        in_specs=[vmem] * 3 + [pl.BlockSpec(memory_space=pl.ANY)],
        out_specs=[vmem, vmem],
        out_shape=[
            jax.ShapeDtypeStruct((4, PTS, 8, NCOL), F32),
            jax.ShapeDtypeStruct((4, PTS, 8, NCOL), BF),
        ],
        scratch_shapes=[
            pltpu.VMEM((STEPS * ROWS, NCOL), F32),
            pltpu.VMEM((FREQ * ROWS, NCOL), F32),
            pltpu.VMEM((PTS * FREQ, NCOL), F32),
            pltpu.VMEM(spectra.shape, BF),
            pltpu.SemaphoreType.DMA,
        ],
        compiler_params=pltpu.CompilerParams(vmem_limit_bytes=48 << 20),
        name="adjoint",
    )(everything, fwd, inv, spectra)


def forward_kernel(
    mine_ref, other_ref, fwd_ref, inv_ref, spec_ref, out_ref, model_ref, res_ref, spec, sem
):
    copy = pltpu.make_async_copy(spec_ref, spec, sem)
    copy.start()
    high, low = halves(fwd_ref[...])
    fwd = jnp.concatenate([high, low], axis=1)

    def to_bins(i, c):
        values = [
            jnp.concatenate(
                [ref[p, i * 4 + j].astype(F32) for ref in (mine_ref, other_ref) for p in range(4)],
                axis=0,
            ).astype(BF)
            for j in range(4)
        ]
        block = jnp.concatenate(values, axis=1)
        result = dot(fwd, jnp.concatenate([block, block], axis=0))
        for j in range(4):
            model_ref[pl.ds(i * 4 + j, FREQ, stride=PTS), :] = result[:, j * NCOL : (j + 1) * NCOL]
        return c

    lax.fori_loop(0, PTS // 4, to_bins, 0)
    copy.wait()
    sensors = spec.shape[2]
    zero = jnp.zeros((ROWS, NCOL), F32)
    for j in range(2 * NB, FREQ):
        res_ref[pl.ds(j, ROWS, stride=FREQ), :] = zero
    pad = jnp.zeros((ROWS - sensors, 2 * NCOL), F32)

    def one_bin(k):
        real = model_ref[pl.ds(pl.multiple_of(k * PTS, 8), PTS), :].astype(BF)
        imag = model_ref[pl.ds(pl.multiple_of((k + NB) * PTS, 8), PTS), :].astype(BF)
        result = dot(spec[0, k], jnp.concatenate([real, imag], axis=1)) + dot(
            spec[1, k], jnp.concatenate([-imag, real], axis=1)
        )
        result = jnp.concatenate([result, pad], axis=0)
        res_ref[pl.ds(k, ROWS, stride=FREQ), :] = result[:, :NCOL]
        res_ref[pl.ds(k + NB, ROWS, stride=FREQ), :] = result[:, NCOL:]

    def five_bins(i, c):
        for j in range(5):
            one_bin(i * 5 + j)
        return c

    lax.fori_loop(0, NB // 5, five_bins, 0)

    high, low = halves(inv_ref[...])
    inv = jnp.concatenate([high, high, low], axis=1)

    def to_steps(i, c):
        values = [
            res_ref[pl.ds(pl.multiple_of((i * 4 + j) * FREQ, 8), FREQ), :] for j in range(4)
        ]
        top, rest = halves(jnp.concatenate(values, axis=1))
        result = dot(inv, jnp.concatenate([top, rest, top], axis=0))
        for j in range(4):
            model_ref[pl.ds(i * 4 + j, STEPS, stride=ROWS), :] = result[:, j * NCOL : (j + 1) * NCOL]
        return c

    lax.fori_loop(0, ROWS // 4, to_steps, 0)
    for i in range(STEPS):
        out_ref[i] = model_ref[pl.ds(i * ROWS, ROWS), :].astype(BF)


def forward_map(mine, other, fwd, inv, spectra):
    vmem = pl.BlockSpec(memory_space=pltpu.VMEM)
    return pl.pallas_call(
        forward_kernel,
        in_specs=[vmem] * 4 + [pl.BlockSpec(memory_space=pl.ANY)],
        out_specs=vmem,
        out_shape=jax.ShapeDtypeStruct((STEPS, ROWS, NCOL), BF),
        scratch_shapes=[
            pltpu.VMEM((FREQ * PTS, NCOL), F32),
            pltpu.VMEM((ROWS * FREQ, NCOL), F32),
            pltpu.VMEM(spectra.shape, BF),
            pltpu.SemaphoreType.DMA,
        ],
        compiler_params=pltpu.CompilerParams(vmem_limit_bytes=48 << 20),
        name="forward_map",
    )(mine, other, fwd, inv, spectra)


def shards(readings, spectra, stiffness):
    yh, core = lax.axis_index("yh"), lax.axis_index("core")
    sensors = readings.shape[1]
    by_place = np.arange(STEPS).reshape(4, 8, 2).transpose(0, 2, 1).reshape(-1)
    halves_of = [np.arange(STEPS), np.roll(np.arange(STEPS), 32)]
    fwd_f = jnp.where(core == 0, *[jnp.asarray(forward_table(s)) for s in halves_of])
    inv_f = jnp.where(core == 0, *[jnp.asarray(inverse_table(s)) for s in halves_of])

    chain = [(i, i + 1) for i in range(31)]
    back = [(i + 1, i) for i in range(31)]
    swap = [(0, 1), (1, 0)]
    other = lax.ppermute(stiffness, "yh", swap)
    coeff = jnp.where(
        yh == 0, jnp.concatenate([stiffness, other]), jnp.concatenate([other, stiffness])
    )
    coeff = jnp.concatenate(
        [
            lax.ppermute(coeff[-GY:], ("x", "z"), chain),
            coeff,
            lax.ppermute(coeff[:GY], ("x", "z"), back),
        ]
    ).reshape(6, GY)

    column = jnp.pad(readings, ((0, 0), (0, ROWS - sensors), (0, 0)))
    column = lax.all_gather(column, "z", axis=0, tiled=True)
    column = jnp.broadcast_to(column[None], (8,) + column.shape).reshape(STEPS, ROWS, NCOL)
    everything = lax.all_to_all(column, ("x", "yh"), 0, 0, tiled=True)
    keep, give = adjoint(everything, jnp.asarray(forward_table(by_place)), inv_f, spectra)

    field = (keep + lax.ppermute(give, "core", swap).astype(F32)).astype(BF)
    field = lax.all_to_all(field, ("yh", "yl"), 0, 0, tiled=True).astype(F32)
    field = field.reshape(2, 2, PTS, 8, NCOL)
    grid = (field[:, 0] + field[:, 1]).reshape(4, GY, 8, NCOL)
    low = lax.ppermute(grid[-2:].astype(BF), ("x", "z"), chain)
    high = lax.ppermute(grid[:2].astype(BF), ("x", "z"), back)
    grid = jnp.concatenate([low.astype(F32), grid, high.astype(F32)])
    for sweep in range(2):
        inner = grid[1:-1]
        sides = jnp.pad(inner, ((0, 0), (1, 1), (0, 0), (0, 0)))
        beside = grid[:-2] + grid[2:] + sides[:, :-2] + sides[:, 2:]
        rows = coeff if sweep == 0 else coeff[1:-1]
        grid = inner + rows[:, :, None, None] * (beside - 4.0 * inner)
    grid = grid.astype(BF).reshape(2, 1, PTS, 8, NCOL)
    grid = jnp.broadcast_to(grid, (2, 2, PTS, 8, NCOL)).reshape(4, PTS, 8, NCOL)
    mine = lax.all_to_all(grid, ("yh", "yl"), 0, 0, tiled=True)
    other = lax.ppermute(mine, "core", swap)

    out = forward_map(mine, other, fwd_f, jnp.asarray(inverse_table(by_place)), spectra)
    out = lax.all_to_all(out, ("x", "yh"), 0, 0, tiled=True).astype(F32)
    out = jnp.sum(out.reshape(8, 8, ROWS, NCOL), axis=0).astype(BF)
    out = lax.all_to_all(out, "z", 0, 0, tiled=True).astype(F32)
    return jnp.sum(out, axis=0, keepdims=True)[:, :sensors]


def solution(mesh):
    fine = Mesh(mesh.devices.reshape(4, 8, 2, 2, 2), ("x", "z", "yh", "yl", "core"))
    param, sensor = ("x", "z", "yh"), ("yl", "core")
    return jax.shard_map(
        shards,
        mesh=fine,
        in_specs=(P(param, sensor, None), P(None, None, sensor, param), P(param)),
        out_specs=P(param, sensor, None),
        check_vma=False,
    )
```

time: 816 us -> 222 us (0.27)
  waiting for transfers between devices: 673 us -> 43.8 us
  blocking collectives: 0 us -> 97.8 us
  matrix products: 61 us -> 0 us
  Pallas kernels: 0 us -> 42.5 us
  local copies, waits for them, and re-layouts: 36.2 us -> 9.25 us
  between operations: 13.8 us -> 0.21 us
  starting transfers between devices: 14.6 us -> 23.9 us
    unnamed x4 -> x0, waiting for transfers between devices: 382 us -> none
    all_gather x1 -> x0, waiting for transfers between devices: 112 us -> none  [shards(): lax.all_gather(readings, 'param', axis=0, tiled=True)]
    psum x1 -> x0, waiting for transfers between devices: 92.4 us -> none  [shards(): grid = lax.psum(grid, 'sensor')]
    all_to_all x0 -> x3, blocking collectives: none -> 69.1 us  [the longest x1 37.7 us: shards(): out = lax.all_to_all(out, ('x', 'yh'), 0, 0, tiled=True).astype(F32)]
    ppermute x4 -> x7, waiting for transfers between devices: 86.6 us -> 21.2 us  [the longest x1 11.9 us: shards(): other = lax.ppermute(stiffness, 'yh', swap)]
    dot_general x16 -> x0, matrix products: 61 us -> none  [the longest x2 11.6 us: inverse_rows(): jnp.einsum('ni,ilj->nlj', cosine_inverse, real_part, precision=hessian_pr...]
    pallas_call x0 -> x2, Pallas kernels: none -> 42.5 us  [the longest x1 22.8 us: forward_map(): pl.pallas_call(forward_kernel, in_specs=[vmem] * 4 + [pl.BlockSpec(memory...]
    all_gather x0 -> x1, blocking collectives: none -> 28.7 us  [shards(): column = lax.all_gather(column, 'z', axis=0, tiled=True)]
  transfers between devices with their start and end apart: 7 -> 9, of which waited for: 5 -> 5; matrix products, arithmetic and copies ran while one was open for 2% -> 3% of each run, Pallas kernels for 0% -> 0%
where the time goes in v1:
time: 222 us; the launch traced here: 221 us
  blocking collectives  97.8 us (44%)
  waiting for transfers between devices  43.8 us (20%)
  Pallas kernels  42.5 us (19%)
  starting transfers between devices  23.9 us (11%)
  local copies, waits for them, and re-layouts  9.25 us (4%)
  other arithmetic  3.5 us (2%)
    all_to_all x1, blocking collectives, shards(): out = lax.all_to_all(out, ('x', 'yh'), 0, 0, tiled=True).astype(F32)  37.7 us
    all_gather x1, blocking collectives, shards(): column = lax.all_gather(column, 'z', axis=0, tiled=True)  28.7 us
    pallas_call x1, Pallas kernels, forward_map(): pl.pallas_call(forward_kernel, in_specs=[vmem] * 4 + [pl.BlockSpec(memory...  22.8 us
    all_to_all x1, waiting for transfers between devices, shards(): everything = lax.all_to_all(column, ('x', 'yh'), 0, 0, tiled=True)  22.5 us
    pallas_call x1, Pallas kernels, adjoint(): pl.pallas_call(adjoint_kernel, in_specs=[vmem] * 3 + [pl.BlockSpec(memory...  19.7 us
    all_to_all x1, blocking collectives, shards(): out = lax.all_to_all(out, 'z', 0, 0, tiled=True).astype(F32)  16.2 us
    all_to_all x1, blocking collectives, shards(): mine = lax.all_to_all(grid, ('yh', 'yl'), 0, 0, tiled=True)  15.2 us
    ppermute x1, waiting for transfers between devices, shards(): other = lax.ppermute(stiffness, 'yh', swap)  11.9 us
  transfers between devices with their start and end apart: 9, of which 5 were waited for; matrix products, arithmetic and copies ran while one was open for 3% of the time, Pallas kernels for 0%

profile of v1, /device:TPU:8, one launch (start us, length us, event | category | flops | bytes accessed | tf_op | source)
XLA Modules:
  0.0 221.0 jit_solution(17056439799670517293)
XLA Ops:
  0.0 0.8 pad.12
  0.8 28.7 %all_gather.3 = bf16[8,152,128]{2,1,0:T(8,128)(2,1)S(1)} all-gather(bf16[1,152,128]{2,1,0:T(8,128)(2,1)S(1)} %pad.12), channel_id=1, replica_groups=mesh['x'=4,'z'=8,'yh'=2,'yl'=2,'core'=2] {'z'}, dimensions={0}, use_global_device_ids=true | all-gather | bytes 350208 | tf_op jit(solution)/shard_map/all_gather | solution.py:237
  29.5 1.8 broadcast_in_dim.8
  31.3 6.0 %all-to-all-start = ((bf16[64,152,128]{2,1,0:T(8,128)(2,1)}), bf16[64,152,128]{2,1,0:T(8,128)(2,1)S(1)}, u32[]{:S(2)}, u32[]{:S(2)}) async-start(bf16[64,152,128]{2,1,0:T(8,128)(2,1)} %bitcast.11), calls=%async_computation | async-start | bytes 4980736 | tf_op jit(solution)/shard_map/all_to_all | solution.py:239
  37.3 0.0 copy-start.5
  37.3 0.0 copy-start
  37.3 5.4 %copy.14.spec_ref = bf16[2,65,150,128]{3,2,1,0:T(8,128)(2,1)} copy(bf16[2,65,150,128]{3,0,2,1:T(2,128)(2,1)} %param.10) | data formatting | bytes 9984000 | tf_op args[1]
  42.7 0.0 copy-done.5
  42.7 22.5 %all-to-all-done.read_ref = bf16[64,152,128]{2,1,0:T(8,128)(2,1)S(1)} async-done(((bf16[64,152,128]{2,1,0:T(8,128)(2,1)}), bf16[64,152,128]{2,1,0:T(8,128)(2,1)S(1)}, u32[]{:S(2)}, u32[]{:S(2)}) %all-to-all-start) | async-done | bytes 2490400 | tf_op jit(solution)/shard_map/all_to_all | solution.py:239
  65.3 19.7 %adjoint.1 = (f32[4,128,8,128]{3,2,1,0:T(8,128)S(1)}, bf16[4,128,8,128]{3,2,1,0:T(8,128)(2,1)S(1)}) custom-call(bf16[64,152,128]{2,1,0:T(8,128)(2,1)S(1)} %all-to-all-done.read_ref, f32[136,64]{1,0:T(8,128)S(1)} %copy-done, f32[64,136]{1,0:T(8,128)S(1)} %broadcast_select_fusion.1.inv_ref, bf16[2,65,150,128]{3,2,1,0:T(8,128)(2,1)} %copy.14.spec_ref), custom_call_target="tpu_custom_call" | custom-call | tf_op jit(solution)/shard_map/adjoint/pallas_call | solution.py:110
  85.0 0.1 collective-permute-start
  85.1 2.6 %collective-permute-done = bf16[4,128,8,128]{3,2,1,0:T(8,128)(2,1)S(1)} collective-permute-done((bf16[4,128,8,128]{3,2,1,0:T(8,128)(2,1)S(1)}, bf16[4,128,8,128]{3,2,1,0:T(8,128)(2,1)S(1)}, u32[]{:S(2)}, u32[]{:S(2)}) %collective-permute-start) | collective-permute-done | bytes 1048608 | tf_op jit(solution)/shard_map/ppermute | solution.py:242
  87.7 1.3 add_convert_fusion
  89.0 5.8 %all-to-all-start.1 = ((bf16[4,128,8,128]{3,2,1,0:T(8,128)(2,1)}), bf16[4,128,8,128]{3,2,1,0:T(8,128)(2,1)S(1)}, u32[]{:S(2)}, u32[]{:S(2)}) async-start(bf16[4,128,8,128]{3,2,1,0:T(8,128)(2,1)} %add_convert_fusion), calls=%async_computation.1 | async-start | bytes 2097152 | tf_op jit(solution)/shard_map/all_to_all | solution.py:243
  94.8 2.1 collective-permute-start.3
  96.8 0.1 concatenate.34
  96.9 11.9 %collective-permute-done.3 = f32[128]{0:T(128)S(1)} collective-permute-done((f32[128]{0:T(128)S(1)}, f32[128]{0:T(128)S(1)}, u32[]{:S(2)}, u32[]{:S(2)}) %collective-permute-start.3) | collective-permute-done | bytes 544 | tf_op jit(solution)/shard_map/ppermute | solution.py:224
  108.8 0.0 all-to-all-done.1
  108.8 0.1 convert.8
  109.0 0.1 fusion.11
  109.2 2.8 %collective-permute-start.1 = (bf16[2,64,8,128]{3,2,1,0:T(8,128)(2,1)S(1)}, bf16[2,64,8,128]{3,2,1,0:T(8,128)(2,1)S(1)}, u32[]{:S(2)}, u32[]{:S(2)}) collective-permute-start(bf16[2,64,8,128]{3,2,1,0:T(8,128)(2,1)S(1)} %bitcast.20), channel_id=1, source_target_pairs={{0,8},{8,16},{16,24},{24,32},{32,40},{40,48},{48,56},{56,64},{64,7... | collective-permute-start | bytes 786440 | tf_op jit(solution)/shard_map/ppermute | solution.py:246
  112.0 1.3 collective-permute-start.2
  113.3 0.1 fusion.13
  113.4 4.5 %collective-permute-start.4 = (f32[64]{0:T(128)S(1)}, f32[64]{0:T(128)S(1)}, u32[]{:S(2)}, u32[]{:S(2)}) collective-permute-start(f32[64]{0:T(128)S(1)} %get-tuple-element.13), channel_id=1, source_target_pairs={{0,8},{8,16},{16,24},{24,32},{32,40},{40,48},{48,56},{56,64},{64,7... | collective-permute-start | bytes 776 | tf_op jit(solution)/shard_map/ppermute | solution.py:230
  117.9 1.3 collective-permute-start.5
  119.2 0.1 concatenate.35
  119.3 0.0 collective-permute-done.4
  119.3 4.1 %collective-permute-done.5 = f32[64]{0:T(128)S(1)} collective-permute-done((f32[64]{0:T(128)S(1)}, f32[64]{0:T(128)S(1)}, u32[]{:S(2)}, u32[]{:S(2)}) %collective-permute-start.5) | collective-permute-done | bytes 288 | tf_op jit(solution)/shard_map/ppermute | solution.py:232
  123.4 0.1 pad_maximum_fusion.2
  123.5 0.1 mul.30
  123.5 0.0 collective-permute-done.1
  123.6 0.0 collective-permute-done.2
  123.6 0.1 pad_maximum_fusion
  123.8 0.9 fusion.4
  124.6 0.1 slice.78
  124.7 0.4 fusion.10
  125.1 0.0 copy-start.2
  125.1 0.0 copy-start.3
  125.1 0.0 copy-start.1
  125.1 0.1 broadcast_in_dim.19
  125.3 15.2 %all_to_all.25.mine_ref = bf16[4,128,8,128]{3,2,1,0:T(8,128)(2,1)S(1)} all-to-all(bf16[4,128,8,128]{3,2,1,0:T(8,128)(2,1)S(1)} %bitcast.16), channel_id=1, replica_groups=mesh['x'=4,'z'=8,'yh'=2,'yl'=2,'core'=2] {'yh','yl'}, dimensions={0} | all-to-all | bytes 2097152 | tf_op jit(solution)/shard_map/all_to_all | solution.py:257
  140.5 0.0 collective-permute-start.6
  140.5 2.6 %collective-permute-done.6.other_ref = bf16[4,128,8,128]{3,2,1,0:T(8,128)(2,1)S(1)} collective-permute-done((bf16[4,128,8,128]{3,2,1,0:T(8,128)(2,1)S(1)}, bf16[4,128,8,128]{3,2,1,0:T(8,128)(2,1)S(1)}, u32[]{:S(2)}, u32[]{:S(2)}) %collective-permute-start.6) | collective-permute-done | bytes 1048608 | tf_op jit(solution)/shard_map/ppermute | solution.py:258
  143.1 22.8 %forward_map.1 = bf16[64,152,128]{2,1,0:T(8,128)(2,1)S(1)} custom-call(bf16[4,128,8,128]{3,2,1,0:T(8,128)(2,1)S(1)} %all_to_all.25.mine_ref, bf16[4,128,8,128]{3,2,1,0:T(8,128)(2,1)S(1)} %collective-permute-done.6.other_ref, f32[136,64]{1,0:T(8,128)S(1)} %broadcast_select_fusion.fwd_ref, f32[64,136]{1,0:T(8,128)S(1)} %copy-done.1, ...), custom_call_target="tpu_custom_call" | custom-call | tf_op jit(solution)/shard_map/forward_map/pallas_call | solution.py:197
  165.9 37.7 %all_to_all.26 = bf16[64,152,128]{2,1,0:T(8,128)(2,1)S(1)} all-to-all(bf16[64,152,128]{2,1,0:T(8,128)(2,1)S(1)} %forward_map.1), channel_id=1, replica_groups=mesh['x'=4,'z'=8,'yh'=2,'yl'=2,'core'=2] {'x','yh'}, dimensions={0} | all-to-all | bytes 4980736 | tf_op jit(solution)/shard_map/all_to_all | solution.py:261
  203.6 0.4 reduce
  204.0 16.2 %all_to_all.27 = bf16[8,152,128]{2,1,0:T(8,128)(2,1)S(1)} all-to-all(bf16[8,152,128]{2,1,0:T(8,128)(2,1)S(1)} %reduce), channel_id=1, replica_groups=mesh['x'=4,'z'=8,'yh'=2,'yl'=2,'core'=2] {'z'}, dimensions={0} | all-to-all | bytes 622592 | tf_op jit(solution)/shard_map/all_to_all | solution.py:263
  220.3 0.7 copy.16
  (16 shorter events, 0.2 us)
Async XLA Ops:
  31.3 34.0 %all-to-all-start = ((bf16[64,152,128]{2,1,0:T(8,128)(2,1)}), bf16[64,152,128]{2,1,0:T(8,128)(2,1)S(1)}, u32[]{:S(2)}, u32[]{:S(2)}) async-start(bf16[64,152,128]{2,1,0:T(8,128)(2,1)} %bitcast.11), calls=%async_computation | async-start | bytes 4980736 | tf_op jit(solution)/shard_map/all_to_all | solution.py:239
  37.3 5.4 %copy-start.4 = (f32[64,136]{1,0:T(8,128)S(1)}, f32[64,136]{1,0:T(8,128)}, u32[]{:S(2)}) copy-start(f32[64,136]{1,0:T(8,128)} %constant.32.clone) | copy-start | bytes 104452
  37.3 5.4 %copy-start.5 = (f32[64,136]{1,0:T(8,128)S(1)}, f32[64,136]{1,0:T(8,128)}, u32[]{:S(2)}) copy-start(f32[64,136]{1,0:T(8,128)} %constant.33.clone) | copy-start | bytes 104452
  37.3 27.9 %copy-start = (f32[136,64]{1,0:T(8,128)S(1)}, f32[136,64]{1,0:T(8,128)}, u32[]{:S(2)}) copy-start(f32[136,64]{1,0:T(8,128)} %constant.34.clone.fwd_ref) | copy-start | bytes 104452
  85.0 2.7 %collective-permute-start = (bf16[4,128,8,128]{3,2,1,0:T(8,128)(2,1)S(1)}, bf16[4,128,8,128]{3,2,1,0:T(8,128)(2,1)S(1)}, u32[]{:S(2)}, u32[]{:S(2)}) collective-permute-start(bf16[4,128,8,128]{3,2,1,0:T(8,128)(2,1)S(1)} %get-tuple-element.8), channel_id=1, source_target_pairs={{0,1},{1,0},{2,3},{3,2},{4,5},{5,4},{6,7},{7,6},{8,9},{9,8},{10,11... | collective-permute-start | bytes 3145736 | tf_op jit(solution)/shard_map/ppermute | solution.py:242
  89.0 5.8 %copy-start.6 = (f32[128]{0:T(128)S(1)}, f32[128]{0:T(128)}, u32[]{:S(2)}) copy-start(f32[128]{0:T(128)} %param.11) | copy-start | bytes 1540
  89.0 19.8 %all-to-all-start.1 = ((bf16[4,128,8,128]{3,2,1,0:T(8,128)(2,1)}), bf16[4,128,8,128]{3,2,1,0:T(8,128)(2,1)S(1)}, u32[]{:S(2)}, u32[]{:S(2)}) async-start(bf16[4,128,8,128]{3,2,1,0:T(8,128)(2,1)} %add_convert_fusion), calls=%async_computation.1 | async-start | bytes 2097152 | tf_op jit(solution)/shard_map/all_to_all | solution.py:243
  94.8 14.0 %collective-permute-start.3 = (f32[128]{0:T(128)S(1)}, f32[128]{0:T(128)S(1)}, u32[]{:S(2)}, u32[]{:S(2)}) collective-permute-start(f32[128]{0:T(128)S(1)} %copy-done.6), channel_id=1, source_target_pairs={{0,4},{4,0},{1,5},{5,1},{2,6},{6,2},{3,7},{7,3},{8,12},{12,8},{9,1... | collective-permute-start | bytes 1544 | tf_op jit(solution)/shard_map/ppermute | solution.py:224
  109.2 14.4 %collective-permute-start.1 = (bf16[2,64,8,128]{3,2,1,0:T(8,128)(2,1)S(1)}, bf16[2,64,8,128]{3,2,1,0:T(8,128)(2,1)S(1)}, u32[]{:S(2)}, u32[]{:S(2)}) collective-permute-start(bf16[2,64,8,128]{3,2,1,0:T(8,128)(2,1)S(1)} %bitcast.20), channel_id=1, source_target_pairs={{0,8},{8,16},{16,24},{24,32},{32,40},{40,48},{48,56},{56,64},{64,7... | collective-permute-start | bytes 786440 | tf_op jit(solution)/shard_map/ppermute | solution.py:246
  112.0 11.6 %collective-permute-start.2 = (bf16[2,64,8,128]{3,2,1,0:T(8,128)(2,1)S(1)}, bf16[2,64,8,128]{3,2,1,0:T(8,128)(2,1)S(1)}, u32[]{:S(2)}, u32[]{:S(2)}) collective-permute-start(bf16[2,64,8,128]{3,2,1,0:T(8,128)(2,1)S(1)} %bitcast.19), channel_id=1, source_target_pairs={{8,0},{16,8},{24,16},{32,24},{40,32},{48,40},{56,48},{64,56},{72,6... | collective-permute-start | bytes 786440 | tf_op jit(solution)/shard_map/ppermute | solution.py:247
  113.4 5.9 %collective-permute-start.4 = (f32[64]{0:T(128)S(1)}, f32[64]{0:T(128)S(1)}, u32[]{:S(2)}, u32[]{:S(2)}) collective-permute-start(f32[64]{0:T(128)S(1)} %get-tuple-element.13), channel_id=1, source_target_pairs={{0,8},{8,16},{16,24},{24,32},{32,40},{40,48},{48,56},{56,64},{64,7... | collective-permute-start | bytes 776 | tf_op jit(solution)/shard_map/ppermute | solution.py:230
  117.9 5.5 %collective-permute-start.5 = (f32[64]{0:T(128)S(1)}, f32[64]{0:T(128)S(1)}, u32[]{:S(2)}, u32[]{:S(2)}) collective-permute-start(f32[64]{0:T(128)S(1)} %get-tuple-element.14), channel_id=1, source_target_pairs={{8,0},{16,8},{24,16},{32,24},{40,32},{48,40},{56,48},{64,56},{72,6... | collective-permute-start | bytes 776 | tf_op jit(solution)/shard_map/ppermute | solution.py:232
  125.1 15.4 %copy-start.2 = (f32[136,64]{1,0:T(8,128)S(1)}, f32[136,64]{1,0:T(8,128)}, u32[]{:S(2)}) copy-start(f32[136,64]{1,0:T(8,128)} %constant.30.clone) | copy-start | bytes 104452
  125.1 15.4 %copy-start.3 = (f32[136,64]{1,0:T(8,128)S(1)}, f32[136,64]{1,0:T(8,128)}, u32[]{:S(2)}) copy-start(f32[136,64]{1,0:T(8,128)} %constant.31.clone) | copy-start | bytes 104452
  125.1 18.0 %copy-start.1 = (f32[64,136]{1,0:T(8,128)S(1)}, f32[64,136]{1,0:T(8,128)}, u32[]{:S(2)}) copy-start(f32[64,136]{1,0:T(8,128)} %constant.35.clone.inv_ref) | copy-start | bytes 104452
  140.5 2.7 %collective-permute-start.6 = (bf16[4,128,8,128]{3,2,1,0:T(8,128)(2,1)S(1)}, bf16[4,128,8,128]{3,2,1,0:T(8,128)(2,1)S(1)}, u32[]{:S(2)}, u32[]{:S(2)}) collective-permute-start(bf16[4,128,8,128]{3,2,1,0:T(8,128)(2,1)S(1)} %all_to_all.25.mine_ref), channel_id=1, source_target_pairs={{0,1},{1,0},{2,3},{3,2},{4,5},{5,4},{6,7},{7,6},{8,9},{9,8},{10,11... | collective-permute-start | bytes 3145736 | tf_op jit(solution)/shard_map/ppermute | solution.py:258
